TPU v7x, 32 devices: a whole 2x2x4 slice. The times are simulated.
32 devices in a mesh: parts: 2 (over y), tile: 4 (over x, core), chan: 4 (over z).
Axes of the slice: x: 2, y: 2, z: 4, core: 2. Of those that a mesh axis runs over, the one named last changes fastest.
Arguments:
- weather: bfloat16 [768, 64, 1440], P('chan', 'parts', 'tile'), parts along dimension 1, may hold values from -6 to 6
- lon_taps: float32 [9, 768], P(None, 'chan'), may hold values from -4 to 4
- latitude_taps: float32 [9, 768], P(None, 'chan'), may hold values from -2 to 2
- norm_gain: float32 [768], replicated, may hold values from 0.1 to 1.9
- up_weight: bfloat16 [768, 3072], P(None, ('tile', 'chan')), may hold values from -0.21875 to 0.21875
- down_weight: bfloat16 [768, 3072], P(None, ('tile', 'chan')), may hold values from -0.109375 to 0.109375
Outputs:
- mixed: bfloat16 [768, 64, 1440], P('chan', 'parts', 'tile'), parts along dimension 1
There are 2 independent parts, one for each index of `parts`. A program takes and returns all parts, laid end to end along the dimension named above; an argument that names none is the same for every part. Nothing has to cross between parts.
All inputs are finite; a program needn't handle non-finite values.
Results may differ from a plain program's by a relative error of at most 0.0065.
Values may be sent and summed in bfloat16 or wider, within the bound.
No kernel may reach another device: no remote copies, remote signals or barrier semaphores. Data moves between devices by JAX's collectives and lax.ppermute only.
A program may use at most 128 MiB of HBM per device.

v0:
```python
import jax
import jax.numpy as jnp
from jax import lax
from jax.sharding import PartitionSpec as P

KERNEL_TAPS = 9
DILATION_STEP = 2


def with_halo(shard, sides, width):
    for axis, dim in sides:
        devices, length = (lax.axis_size(axis), shard.shape[dim])
        up = [(i, (i + 1) % devices) for i in range(devices)]
        down = [(j, i) for i, j in up]
        last = lax.slice_in_dim(shard, length - width, length, axis=dim)
        initial = lax.slice_in_dim(shard, 0, width, axis=dim)
        before = lax.ppermute(last, axis, up)
        after = lax.ppermute(initial, axis, down)
        shard = jnp.concatenate([before, shard, after], axis=dim)
    return shard


def layer_norm(values, norm_gain):
    as_float = values.astype(jnp.float32)
    center = jnp.mean(as_float, axis=0)
    deviation = as_float - center
    spread_sq = jnp.mean(deviation * deviation, axis=0)
    return (deviation * lax.rsqrt(spread_sq + 1e-06) * norm_gain[:, None]).astype(jnp.bfloat16)


def on_device(weather, lon_taps, latitude_taps, norm_gain, up_weight, down_weight):
    chan_count, row_total, column_total = weather.shape
    border_width = DILATION_STEP * (KERNEL_TAPS // 2)
    widened_field = with_halo(weather, (("tile", 2),), border_width)
    lon_sum = jnp.zeros(weather.shape, jnp.float32)
    for kernel_tap_index in range(KERNEL_TAPS):
        sliding_window = widened_field[
            :, :, DILATION_STEP * kernel_tap_index : DILATION_STEP * kernel_tap_index + column_total
        ].astype(jnp.float32)
        lon_sum = lon_sum + lon_taps[kernel_tap_index][:, None, None] * sliding_window
    padded_field = jnp.pad(lon_sum, ((0, 0), (border_width, border_width), (0, 0)))
    latitude_sum = jnp.zeros(weather.shape, jnp.float32)
    for kernel_tap_index in range(KERNEL_TAPS):
        latitude_sum = (
            latitude_sum
            + latitude_taps[kernel_tap_index][:, None, None]
            * padded_field[
                :,
                DILATION_STEP * kernel_tap_index : DILATION_STEP * kernel_tap_index + row_total,
                :,
            ]
        )
    spatial = latitude_sum.astype(jnp.bfloat16)
    group_count = lax.axis_size("chan")
    width_all = chan_count * group_count
    shard_width = up_weight.shape[1]
    by_cell = lax.all_to_all(spatial, "chan", split_axis=1, concat_axis=0, tiled=True)
    cell_count = by_cell.shape[1] * by_cell.shape[2]
    normed = layer_norm(by_cell.reshape(width_all, cell_count), norm_gain)
    expanded = lax.dot_general(
        lax.all_gather(up_weight, ("tile", "chan"), axis=1, tiled=True),
        normed,
        (((0,), (0,)), ((), ())),
        preferred_element_type=jnp.float32,
    )
    hidden = jax.nn.gelu(expanded, approximate=False).astype(jnp.bfloat16)
    down_all = lax.all_gather(down_weight, ("tile", "chan"), axis=1, tiled=True)
    tile_count = down_all.shape[1] // (group_count * shard_width)
    down_groups = down_all.reshape(width_all, tile_count, group_count, shard_width)
    hidden_groups = hidden.reshape(tile_count, group_count, shard_width, cell_count)
    summed = jnp.zeros((width_all, cell_count), jnp.float32)
    for group in range(group_count):
        group_value = jnp.einsum(
            "dts,tsc->dc",
            down_groups[:, :, group, :],
            hidden_groups[:, group],
            preferred_element_type=jnp.float32,
        ).astype(jnp.bfloat16)
        group_value = lax.optimization_barrier(group_value)
        summed = summed + group_value.astype(jnp.float32)
    update_cells = summed.astype(jnp.bfloat16).reshape(width_all, by_cell.shape[1], column_total)
    update = lax.all_to_all(update_cells, "chan", split_axis=0, concat_axis=1, tiled=True)
    return (weather.astype(jnp.float32) + update.astype(jnp.float32)).astype(jnp.bfloat16)


def solution(mesh):
    return jax.shard_map(
        on_device,
        mesh=mesh,
        in_specs=(
            P("chan", "parts", "tile"),
            P(None, "chan"),
            P(None, "chan"),
            P(),
            P(None, ("tile", "chan")),
            P(None, ("tile", "chan")),
        ),
        out_specs=P("chan", "parts", "tile"),
        check_vma=False,
    )
```

profile of v0, /device:TPU:0, one launch (start us, length us, event | category | flops | bytes accessed | tf_op | source)
XLA Modules:
  0.0 563.3 jit_solution(12894988400171444290)
XLA Ops:
  7.3 2.6 fusion.56
  11.2 2.4 collective-permute-start.1
  15.0 4.3 collective-permute-done
  22.0 36.4 %fusion.22 = f32[192,32,360]{2,1,0:T(8,128)} fusion(bf16[192,32,360]{2,1,0:T(8,128)(2,1)} %param.6, bf16[192,32,8]{2,1,0:T(8,128)(2,1)S(1)} %copy.38, bf16[192,32,8]{2,1,0:T(8,128)(2,1)S(1)} %copy.36, f32[192]{0:T(256)S(1)} %bitcast.205, f32[192]{0:T(256)S(1)} %bitcast.206, f32[192]{0:T(256)S(1)} %bitcast.199, f32[192]{0:T(256)S(1)} %bitcast.200, ...), kind=kLoop, calls=%fused_computation.38 | loop fusion | flops 110592000 | bytes 13474560 | tf_op jit(solution)/shard_map/add | solution.py:40
  58.4 34.3 %fusion.33 = bf16[192,32,360]{2,1,0:T(8,128)(2,1)S(1)} fusion(f32[192,32,360]{2,1,0:T(8,128)} %fusion.22, f32[192]{0:T(256)S(1)} %bitcast.196, f32[192]{0:T(256)S(1)} %bitcast.197, f32[192]{0:T(256)S(1)} %bitcast.190, f32[192]{0:T(256)S(1)} %bitcast.191, f32[192]{0:T(256)S(1)} %bitcast.192, f32[192]{0:T(256)S(1)} %bitcast.193, f32[192]{0:T(256)S(1)} %bitcast.194, ...), kind=kLoop, calls=%fused_computation.49 | loop fusion | flops 39813120 | bytes 13277952 | tf_op jit(solution)/shard_map/convert_element_type | solution.py:53
  92.7 4.0 copy.39
  96.7 5.0 all-to-all-start
  102.4 130.9 %all-to-all-done = bf16[192,32,360]{2,0,1:T(8,128)(2,1)} async-done(((bf16[192,32,360]{2,0,1:T(8,128)(2,1)}), bf16[192,32,360]{2,0,1:T(8,128)(2,1)}, u32[]{:S(2)}, u32[]{:S(2)}) %all-to-all-start) | async-done | bytes 4423712 | tf_op jit(solution)/shard_map/all_to_all | solution.py:57
  233.2 3.5 bitcast_convert_fusion.4
  236.7 5.0 fusion.55
  241.7 9.1 %copy.68 = f32[192,4,8,360]{3,2,0,1:T(8,128)} copy(f32[192,4,8,360]{3,0,2,1:T(8,128)S(1)} %bitcast_convert_fusion.4) | data formatting | bytes 17694720 | tf_op jit(solution)/shard_map/convert_element_type | solution.py:24
  250.8 5.0 multiply_reduce_fusion
  255.9 11.5 %reshape.71 = f32[768,2880]{1,0:T(8,128)} reshape(f32[4,192,8,360]{3,2,1,0:T(8,128)} %bitcast.180) | data formatting | bytes 17694720 | tf_op jit(solution)/shard_map/convert_element_type | solution.py:24
  267.5 7.2 %multiply_convert_fusion.1.clone.4 = bf16[768,2880]{1,0:T(8,128)(2,1)} fusion(f32[768,2880]{1,0:T(8,128)} %reshape.71, f32[768]{0:T(1024)S(1)} %copy-done.3, f32[2880]{0:T(1024)S(1)} %rsqrt.11, f32[2880]{0:T(1024)S(1)} %div.9), kind=kLoop, calls=%fused_computation.60.clone.clone.clone.clone.1 | loop fusion | flops 8847360 | bytes 13297152 | tf_op jit(solution)/shard_map/convert_element_type | solution.py:66
  274.7 102.8 %fusion.2 = bf16[3072,2880]{0,1:T(8,128)(2,1)} fusion(bf16[768,3072]{0,1:T(8,128)(2,1)} %all-gather.3.cloned.1.call-done, bf16[768,2880]{1,0:T(8,128)(2,1)} %multiply_convert_fusion.1.clone.4), kind=kOutput, calls=%fused_computation.3 | convolution fusion | flops 14164623360 | bytes 26836992 | tf_op jit(solution)/shard_map/dot_general | solution.py:60
  377.5 22.1 %copy.41 = bf16[3072,2880]{1,0:T(8,128)(2,1)} copy(bf16[3072,2880]{0,1:T(8,128)(2,1)} %fusion.2) | data formatting | bytes 35389440 | tf_op jit(solution)/shard_map/convert_element_type | solution.py:66
  399.7 8.7 %fusion.53 = bf16[768,2880]{0,1:T(8,128)(2,1)} fusion(bf16[4,4,192,2880]{3,2,1,0:T(8,128)(2,1)} %bitcast.184, bf16[768,4,4,192]{0,3,2,1:T(8,128)(2,1)} %bitcast.207), kind=kOutput, calls=%fused_computation.92 | convolution fusion | flops 3399598080 | bytes 10125312 | tf_op jit(solution)/shard_map/dts,tsc->dc/dot_general | solution.py:73
  410.5 5.5 fusion.52
  415.9 5.6 fusion.51
  421.5 5.7 %fusion.54 = bf16[768,2880]{0,1:T(8,128)(2,1)} fusion(bf16[4,4,192,2880]{3,2,1,0:T(8,128)(2,1)S(1)} %bitcast.187, bf16[768,4,4,192]{0,3,2,1:T(8,128)(2,1)S(1)} %bitcast.210), kind=kOutput, calls=%fused_computation.93 | convolution fusion | flops 3399598080 | bytes 10125312 | tf_op jit(solution)/shard_map/dts,tsc->dc/dot_general | solution.py:73
  427.2 10.3 %add_convert_fusion = bf16[768,2880]{0,1:T(8,128)(2,1)} fusion(bf16[768,2880]{0,1:T(8,128)(2,1)} %fusion.54, bf16[768,2880]{0,1:T(8,128)(2,1)} %fusion.53, bf16[768,2880]{0,1:T(8,128)(2,1)} %fusion.52, bf16[768,2880]{0,1:T(8,128)(2,1)} %fusion.51), kind=kLoop, calls=%fused_computation.65 | loop fusion | flops 17694720 | bytes 22118400 | tf_op jit(solution)/shard_map/convert_element_type | solution.py:81
  437.6 7.0 %copy.50 = bf16[768,8,360]{2,1,0:T(8,128)(2,1)} copy(bf16[768,8,360]{0,2,1:T(8,128)(2,1)} %bitcast.188) | data formatting | bytes 8847360 | tf_op jit(solution)/shard_map/reshape | solution.py:81
  444.5 108.1 %all_to_all.8 = bf16[768,8,360]{2,1,0:T(8,128)(2,1)S(1)} all-to-all(bf16[768,8,360]{2,1,0:T(8,128)(2,1)} %copy.50), channel_id=1, replica_groups=mesh['parts'=2,'tile'=4,'chan'=4] {'chan'}, dimensions={0} | all-to-all | bytes 8847360 | tf_op jit(solution)/shard_map/all_to_all | solution.py:82
  552.7 3.4 fusion.23
  (33 shorter events, 9.0 us)
Async XLA Ops:
  6.5 8.4 %copy-start.1 = (f32[9,192]{1,0:T(8,128)S(1)}, f32[9,192]{1,0:T(8,128)}, u32[]{:S(2)}) copy-start(f32[9,192]{1,0:T(8,128)} %param.7) | copy-start | bytes 20740
  6.5 8.4 %copy-start.2 = (f32[9,192]{1,0:T(8,128)S(1)}, f32[9,192]{1,0:T(8,128)}, u32[]{:S(2)}) copy-start(f32[9,192]{1,0:T(8,128)} %param.8) | copy-start | bytes 20740
  6.5 268.1 %all-gather.3.cloned.1.call-start = ((), (), s32[]{:S(2)}) async-start(), calls=%async_computation.2 | async-start | bytes 5013504 | tf_op jit(solution)/shard_map/all_gather | solution.py:61
  11.2 9.5 %collective-permute-start.1 = (bf16[192,32,8]{0,2,1:T(8,128)(2,1)S(1)}, bf16[192,32,8]{0,2,1:T(8,128)(2,1)S(1)}, u32[]{:S(2)}, u32[]{:S(2)}) collective-permute-start(bf16[192,32,8]{0,2,1:T(8,128)(2,1)S(1)} %copy.53), channel_id=1, source_target_pairs={{4,0},{8,4},{12,8},{0,12},{5,1},{9,5},{13,9},{1,13},{6,2},{10,6},{... | collective-permute-start | bytes 294920 | tf_op jit(solution)/shard_map/ppermute | solution.py:18
  14.9 4.4 collective-permute-start
  96.7 136.6 %all-to-all-start = ((bf16[192,32,360]{2,0,1:T(8,128)(2,1)}), bf16[192,32,360]{2,0,1:T(8,128)(2,1)}, u32[]{:S(2)}, u32[]{:S(2)}) async-start(bf16[192,32,360]{2,0,1:T(8,128)(2,1)} %copy.39), calls=%async_computation | async-start | bytes 9437184 | tf_op jit(solution)/shard_map/all_to_all | solution.py:57
  101.6 298.0 %all-gather.5.cloned.1.call-start = ((), (), s32[]{:S(2)}) async-start(), calls=%async_computation.3 | async-start | bytes 5013504 | tf_op jit(solution)/shard_map/all_gather | solution.py:67
  255.8 11.7 %copy-start.3 = (f32[768]{0:T(1024)S(1)}, f32[768]{0:T(1024)}, u32[]{:S(2)}) copy-start(f32[768]{0:T(1024)} %param.9) | copy-start | bytes 9220
  399.7 8.8 %copy-start = (bf16[3072,2880]{1,0:T(8,128)(2,1)S(1)}, bf16[3072,2880]{1,0:T(8,128)(2,1)}, u32[]{:S(2)}) copy-start(bf16[3072,2880]{1,0:T(8,128)(2,1)} %copy.41) | copy-start | bytes 53084164
  399.7 10.8 %copy-start.4 = (bf16[768,3072]{0,1:T(8,128)(2,1)S(1)}, bf16[768,3072]{0,1:T(8,128)(2,1)}, u32[]{:S(2)}) copy-start(bf16[768,3072]{0,1:T(8,128)(2,1)} %all-gather.5.cloned.1.call-done) | copy-start | bytes 14155780
  437.6 115.1 %slice-start = ((s8[4718592]{0:T(1024)(128)(4,1)}), s8[524288]{0:T(1024)(128)(4,1)S(1)}, s32[]{:S(2)}) async-start(s8[4718592]{0:T(1024)(128)(4,1)} %bitcast.181), calls=%async_computation.4 | async-start | bytes 1048576
  444.5 108.1 %slice-start.1 = ((s8[4718592]{0:T(1024)(128)(4,1)}), s8[4194304]{0:T(1024)(128)(4,1)S(1)}, s32[]{:S(2)}) async-start(s8[4718592]{0:T(1024)(128)(4,1)} %bitcast.181), calls=%async_computation.5 | async-start | bytes 8388608
Sparse Core Ops, SparseCore 0:
  9.7 56.0 all-gather.2
  104.8 103.3 all-gather.4
where the time goes:
time: 572 us; the launch traced here: 563 us
  waiting for transfers between devices  136 us (24%)
  matrix products  128 us (22%)
  blocking collectives  108 us (19%)
  other arithmetic  105 us (18%)
  local copies, waits for them, and re-layouts  63.8 us (11%)
  between operations  14 us (2%)
  starting transfers between devices  7.74 us (1%)
    all_to_all x1, waiting for transfers between devices, on_device(): lax.all_to_all(spatial, 'chan', split_axis=1, concat_axis=0, tiled=True)  131 us
    all_to_all x1, blocking collectives, on_device(): lax.all_to_all(update_cells, 'chan', split_axis=0, concat_axis=1, tiled=T...  108 us
    dot_general x1, matrix products, on_device(): lax.dot_general(lax.all_gather(up_weight, ('tile', 'chan'), axis=1, tiled...  103 us
    add x1, other arithmetic, on_device(): lon_sum + lon_taps[kernel_tap_index][:, None, None] * sliding_window  36.4 us
    convert_element_type x1, other arithmetic, on_device(): spatial = latitude_sum.astype(jnp.bfloat16)  34.3 us
    dot_general x4, matrix products, on_device(): jnp.einsum('dts,tsc->dc', down_groups[:, :, group, :], hidden_groups[:, g...  25.5 us
    convert_element_type x1, local copies, waits for them, and re-layouts, on_device(): hidden = jax.nn.gelu(expanded, approximate=False).astype(jnp.bfloat16)  22.1 us
    convert_element_type x2, local copies, waits for them, and re-layouts, layer_norm(): as_float = values.astype(jnp.float32)  20.6 us
  transfers between devices with their start and end apart: 5, of which 2 were waited for; matrix products, arithmetic and copies ran while one was open for 44% of the time, Pallas kernels for 0%

commit v1 on v0

--- a/solution.py
+++ b/solution.py
@@ -54,7 +54,10 @@
     group_count = lax.axis_size("chan")
     width_all = chan_count * group_count
     shard_width = up_weight.shape[1]
-    by_cell = lax.all_to_all(spatial, "chan", split_axis=1, concat_axis=0, tiled=True)
+    by_cell = jnp.concatenate(
+        lax.all_to_all(jnp.stack(jnp.split(spatial, lax.axis_size("chan"), axis=1)), "chan", 0, 0),
+        axis=0,
+    )
     cell_count = by_cell.shape[1] * by_cell.shape[2]
     normed = layer_norm(by_cell.reshape(width_all, cell_count), norm_gain)
     expanded = lax.dot_general(

time: 572 us -> 544 us (0.951)
  local copies, waits for them, and re-layouts: 63.8 us -> 49.1 us
  starting transfers between devices: 7.74 us -> 21.1 us
  waiting for transfers between devices: 136 us -> 123 us
  matrix products: 128 us -> 118 us
    all_gather x1, starting transfers between devices: 0.3 us -> 13.7 us  [on_device(): down_all = lax.all_gather(down_weight, ('tile', 'chan'), axis=1, tiled=True)]
    all_to_all x1, waiting for transfers between devices: 131 us -> 118 us  [on_device(): lax.all_to_all(jnp.stack(jnp.split(spatial, lax.axis_size('chan'), axis=1...]
    convert_element_type x2 -> x1, local copies, waits for them, and re-layouts: 20.6 us -> 9.67 us  [layer_norm(): as_float = values.astype(jnp.float32)]
    dot_general x1, matrix products: 103 us -> 92.1 us  [on_device(): lax.dot_general(lax.all_gather(up_weight, ('tile', 'chan'), axis=1, tiled...]
  transfers between devices with their start and end apart: 5 -> 5, of which waited for: 2 -> 2; matrix products, arithmetic and copies ran while one was open for 44% -> 41% of each run, Pallas kernels for 0% -> 0%
where the time goes in v1:
time: 544 us; the launch traced here: 535 us
  waiting for transfers between devices  123 us (23%)
  matrix products  118 us (22%)
  blocking collectives  108 us (20%)
  other arithmetic  102 us (19%)
  local copies, waits for them, and re-layouts  49.1 us (9%)
  starting transfers between devices  21.1 us (4%)
  between operations  14 us (3%)
    all_to_all x1, waiting for transfers between devices, on_device(): lax.all_to_all(jnp.stack(jnp.split(spatial, lax.axis_size('chan'), axis=1...  118 us
    all_to_all x1, blocking collectives, on_device(): lax.all_to_all(update_cells, 'chan', split_axis=0, concat_axis=1, tiled=T...  108 us
    dot_general x1, matrix products, on_device(): lax.dot_general(lax.all_gather(up_weight, ('tile', 'chan'), axis=1, tiled...  92.1 us
    add x1, other arithmetic, on_device(): lon_sum + lon_taps[kernel_tap_index][:, None, None] * sliding_window  37 us
    convert_element_type x1, other arithmetic, on_device(): spatial = latitude_sum.astype(jnp.bfloat16)  34.8 us
    dot_general x4, matrix products, on_device(): jnp.einsum('dts,tsc->dc', down_groups[:, :, group, :], hidden_groups[:, g...  25.4 us
    convert_element_type x1, local copies, waits for them, and re-layouts, on_device(): hidden = jax.nn.gelu(expanded, approximate=False).astype(jnp.bfloat16)  21.9 us
    all_gather x1, starting transfers between devices, on_device(): down_all = lax.all_gather(down_weight, ('tile', 'chan'), axis=1, tiled=True)  13.7 us
  transfers between devices with their start and end apart: 5, of which 2 were waited for; matrix products, arithmetic and copies ran while one was open for 41% of the time, Pallas kernels for 0%

profile of v1, /device:TPU:0, one launch (start us, length us, event | category | flops | bytes accessed | tf_op | source)
XLA Modules:
  0.0 535.0 jit_solution(12470610121679659133)
XLA Ops:
  7.3 2.6 fusion.55
  11.2 2.4 collective-permute-start.1
  15.0 4.3 collective-permute-done
  22.0 37.0 %fusion.22 = f32[192,32,360]{2,1,0:T(8,128)} fusion(bf16[192,32,360]{2,1,0:T(8,128)(2,1)} %param.6, bf16[192,32,8]{2,1,0:T(8,128)(2,1)S(1)} %copy.36, bf16[192,32,8]{2,1,0:T(8,128)(2,1)S(1)} %copy.34, f32[192]{0:T(256)S(1)} %bitcast.202, f32[192]{0:T(256)S(1)} %bitcast.203, f32[192]{0:T(256)S(1)} %bitcast.196, f32[192]{0:T(256)S(1)} %bitcast.197, ...), kind=kLoop, calls=%fused_computation.38 | loop fusion | flops 110592000 | bytes 13474560 | tf_op jit(solution)/shard_map/add | solution.py:40
  59.0 34.8 %fusion.33 = bf16[192,32,360]{2,1,0:T(8,128)(2,1)S(1)} fusion(f32[192,32,360]{2,1,0:T(8,128)} %fusion.22, f32[192]{0:T(256)S(1)} %bitcast.193, f32[192]{0:T(256)S(1)} %bitcast.194, f32[192]{0:T(256)S(1)} %bitcast.187, f32[192]{0:T(256)S(1)} %bitcast.188, f32[192]{0:T(256)S(1)} %bitcast.189, f32[192]{0:T(256)S(1)} %bitcast.190, f32[192]{0:T(256)S(1)} %bitcast.191, ...), kind=kLoop, calls=%fused_computation.49 | loop fusion | flops 39813120 | bytes 13277952 | tf_op jit(solution)/shard_map/convert_element_type | solution.py:53
  94.2 2.8 pad_maximum_fusion.2
  97.0 4.9 all-to-all-start
  101.9 13.7 %all-gather.5.cloned.1.call-start = ((), (), s32[]{:S(2)}) async-start(), calls=%async_computation.3 | async-start | bytes 5013504 | tf_op jit(solution)/shard_map/all_gather | solution.py:70
  115.7 117.9 %all-to-all-done = bf16[4,192,8,360]{3,2,1,0:T(8,128)(2,1)} async-done(((bf16[4,192,8,360]{3,2,1,0:T(8,128)(2,1)}), bf16[4,192,8,360]{3,2,1,0:T(8,128)(2,1)}, u32[]{:S(2)}, u32[]{:S(2)}) %all-to-all-start) | async-done | bytes 4423712 | tf_op jit(solution)/shard_map/all_to_all | solution.py:58
  233.6 3.2 convert_reduce_fusion
  236.9 3.7 multiply_reduce_fusion
  240.7 9.7 %reshape.65 = f32[768,2880]{1,0:T(8,128)} reshape(bf16[4,192,8,360]{3,2,1,0:T(8,128)(2,1)} %all-to-all-done) | data formatting | bytes 13271040 | tf_op jit(solution)/shard_map/convert_element_type | solution.py:24
  250.3 7.1 %multiply_convert_fusion.1.clone.4 = bf16[768,2880]{1,0:T(8,128)(2,1)} fusion(f32[768,2880]{1,0:T(8,128)} %reshape.65, f32[768]{0:T(1024)S(1)} %copy-done.3, f32[2880]{0:T(1024)S(1)} %rsqrt.11, f32[2880]{0:T(1024)S(1)} %div.9), kind=kLoop, calls=%fused_computation.59.clone.clone.clone.clone.1 | loop fusion | flops 8847360 | bytes 13297152 | tf_op jit(solution)/shard_map/convert_element_type | solution.py:69
  257.4 92.1 %fusion.2 = bf16[3072,2880]{0,1:T(8,128)(2,1)} fusion(bf16[768,3072]{0,1:T(8,128)(2,1)} %all-gather.3.cloned.1.call-done, bf16[768,2880]{1,0:T(8,128)(2,1)} %multiply_convert_fusion.1.clone.4), kind=kOutput, calls=%fused_computation.3 | convolution fusion | flops 14164623360 | bytes 26836992 | tf_op jit(solution)/shard_map/dot_general | solution.py:63
  349.5 21.9 %copy.37 = bf16[3072,2880]{1,0:T(8,128)(2,1)} copy(bf16[3072,2880]{0,1:T(8,128)(2,1)} %fusion.2) | data formatting | bytes 35389440 | tf_op jit(solution)/shard_map/convert_element_type | solution.py:69
  371.4 8.7 %fusion.53 = bf16[768,2880]{0,1:T(8,128)(2,1)} fusion(bf16[4,4,192,2880]{3,2,1,0:T(8,128)(2,1)} %bitcast.181, bf16[768,4,4,192]{0,3,2,1:T(8,128)(2,1)} %bitcast.204), kind=kOutput, calls=%fused_computation.93 | convolution fusion | flops 3399598080 | bytes 10125312 | tf_op jit(solution)/shard_map/dts,tsc->dc/dot_general | solution.py:76
  380.3 1.9 copy-done.4
  382.2 5.5 %fusion.52 = bf16[768,2880]{0,1:T(8,128)(2,1)} fusion(bf16[4,4,192,2880]{3,2,1,0:T(8,128)(2,1)S(1)} %bitcast.182, bf16[768,4,4,192]{0,3,2,1:T(8,128)(2,1)S(1)} %bitcast.205), kind=kOutput, calls=%fused_computation.92 | convolution fusion | flops 3399598080 | bytes 10125312 | tf_op jit(solution)/shard_map/dts,tsc->dc/dot_general | solution.py:76
  387.7 5.6 %fusion.51 = bf16[768,2880]{0,1:T(8,128)(2,1)} fusion(bf16[4,4,192,2880]{3,2,1,0:T(8,128)(2,1)S(1)} %bitcast.183, bf16[768,4,4,192]{0,3,2,1:T(8,128)(2,1)S(1)} %bitcast.206), kind=kOutput, calls=%fused_computation.91 | convolution fusion | flops 3399598080 | bytes 10125312 | tf_op jit(solution)/shard_map/dts,tsc->dc/dot_general | solution.py:76
  393.2 5.7 %fusion.54 = bf16[768,2880]{0,1:T(8,128)(2,1)} fusion(bf16[4,4,192,2880]{3,2,1,0:T(8,128)(2,1)S(1)} %bitcast.184, bf16[768,4,4,192]{0,3,2,1:T(8,128)(2,1)S(1)} %bitcast.207), kind=kOutput, calls=%fused_computation.94 | convolution fusion | flops 3399598080 | bytes 10125312 | tf_op jit(solution)/shard_map/dts,tsc->dc/dot_general | solution.py:76
  398.9 10.3 %add_convert_fusion = bf16[768,2880]{0,1:T(8,128)(2,1)} fusion(bf16[768,2880]{0,1:T(8,128)(2,1)} %fusion.54, bf16[768,2880]{0,1:T(8,128)(2,1)} %fusion.53, bf16[768,2880]{0,1:T(8,128)(2,1)} %fusion.52, bf16[768,2880]{0,1:T(8,128)(2,1)} %fusion.51), kind=kLoop, calls=%fused_computation.64 | loop fusion | flops 17694720 | bytes 22118400 | tf_op jit(solution)/shard_map/convert_element_type | solution.py:84
  409.3 7.0 %copy.46 = bf16[768,8,360]{2,1,0:T(8,128)(2,1)} copy(bf16[768,8,360]{0,2,1:T(8,128)(2,1)} %bitcast.185) | data formatting | bytes 8847360 | tf_op jit(solution)/shard_map/reshape | solution.py:84
  416.2 108.1 %all_to_all.14 = bf16[768,8,360]{2,1,0:T(8,128)(2,1)S(1)} all-to-all(bf16[768,8,360]{2,1,0:T(8,128)(2,1)} %copy.46), channel_id=1, replica_groups=mesh['parts'=2,'tile'=4,'chan'=4] {'chan'}, dimensions={0} | all-to-all | bytes 8847360 | tf_op jit(solution)/shard_map/all_to_all | solution.py:85
  524.3 3.4 fusion.23
  (32 shorter events, 6.8 us)
Async XLA Ops:
  6.5 8.4 %copy-start.1 = (f32[9,192]{1,0:T(8,128)S(1)}, f32[9,192]{1,0:T(8,128)}, u32[]{:S(2)}) copy-start(f32[9,192]{1,0:T(8,128)} %param.7) | copy-start | bytes 20740
  6.5 8.4 %copy-start.2 = (f32[9,192]{1,0:T(8,128)S(1)}, f32[9,192]{1,0:T(8,128)}, u32[]{:S(2)}) copy-start(f32[9,192]{1,0:T(8,128)} %param.8) | copy-start | bytes 20740
  6.5 250.9 %all-gather.3.cloned.1.call-start = ((), (), s32[]{:S(2)}) async-start(), calls=%async_computation.2 | async-start | bytes 5013504 | tf_op jit(solution)/shard_map/all_gather | solution.py:64
  11.2 9.5 %collective-permute-start.1 = (bf16[192,32,8]{0,2,1:T(8,128)(2,1)S(1)}, bf16[192,32,8]{0,2,1:T(8,128)(2,1)S(1)}, u32[]{:S(2)}, u32[]{:S(2)}) collective-permute-start(bf16[192,32,8]{0,2,1:T(8,128)(2,1)S(1)} %copy.49), channel_id=1, source_target_pairs={{4,0},{8,4},{12,8},{0,12},{5,1},{9,5},{13,9},{1,13},{6,2},{10,6},{... | collective-permute-start | bytes 294920 | tf_op jit(solution)/shard_map/ppermute | solution.py:18
  14.9 4.4 collective-permute-start
  97.0 136.6 %all-to-all-start = ((bf16[4,192,8,360]{3,2,1,0:T(8,128)(2,1)}), bf16[4,192,8,360]{3,2,1,0:T(8,128)(2,1)}, u32[]{:S(2)}, u32[]{:S(2)}) async-start(bf16[4,192,8,360]{3,2,1,0:T(8,128)(2,1)} %pad_maximum_fusion.2), calls=%async_computation | async-start | bytes 9437184 | tf_op jit(solution)/shard_map/all_to_all | solution.py:58
  101.9 269.5 %all-gather.5.cloned.1.call-start = ((), (), s32[]{:S(2)}) async-start(), calls=%async_computation.3 | async-start | bytes 5013504 | tf_op jit(solution)/shard_map/all_gather | solution.py:70
  236.8 13.6 %copy-start.3 = (f32[768]{0:T(1024)S(1)}, f32[768]{0:T(1024)}, u32[]{:S(2)}) copy-start(f32[768]{0:T(1024)} %param.9) | copy-start | bytes 9220
  371.4 8.8 %copy-start = (bf16[3072,2880]{1,0:T(8,128)(2,1)S(1)}, bf16[3072,2880]{1,0:T(8,128)(2,1)}, u32[]{:S(2)}) copy-start(bf16[3072,2880]{1,0:T(8,128)(2,1)} %copy.37) | copy-start | bytes 53084164
  371.4 10.8 %copy-start.4 = (bf16[768,3072]{0,1:T(8,128)(2,1)S(1)}, bf16[768,3072]{0,1:T(8,128)(2,1)}, u32[]{:S(2)}) copy-start(bf16[768,3072]{0,1:T(8,128)(2,1)} %all-gather.5.cloned.1.call-done) | copy-start | bytes 14155780
  409.3 115.1 %slice-start = ((s8[4718592]{0:T(1024)(128)(4,1)}), s8[524288]{0:T(1024)(128)(4,1)S(1)}, s32[]{:S(2)}) async-start(s8[4718592]{0:T(1024)(128)(4,1)} %bitcast.178), calls=%async_computation.4 | async-start | bytes 1048576
  416.2 108.1 %slice-start.1 = ((s8[4718592]{0:T(1024)(128)(4,1)}), s8[4194304]{0:T(1024)(128)(4,1)S(1)}, s32[]{:S(2)}) async-start(s8[4718592]{0:T(1024)(128)(4,1)} %bitcast.178), calls=%async_computation.5 | async-start | bytes 8388608
Sparse Core Ops, SparseCore 0:
  9.7 56.0 all-gather.2
  115.8 114.8 all-gather.4
